TPU v7x, 128 devices: a whole 4x4x4 slice. The times are simulated.
128 devices in a mesh: dp: 4 (over y), dict: 32 (over x, z, core).
Axes of the slice: x: 4, y: 4, z: 4, core: 2. Of those that a mesh axis runs over, the one named last changes fastest.
Arguments:
- acts: bfloat16 [8192, 8192], P('dict', 'dp'), may hold values from -6 to 6
- lists: int32 [512, 2], P('dict'), may hold values from 0 to 31, all different within a row; in each aligned block of 16 rows (0 to 15, 16 to 31, ...) at most 2 rows name the same one
- w_enc: bfloat16 [8192, 32768], P('dp', 'dict'), may hold values from -0.0625 to 0.0625
- w_dec: bfloat16 [32768, 8192], P('dict', 'dp'), may hold values from -0.1875 to 0.1875
- b_enc: bfloat16 [32768], P('dict'), may hold values from -3 to 3
- b_dec: bfloat16 [8192], P('dp'), may hold values from -3 to 3
Outputs:
- grad_enc: bfloat16 [8192, 32768], P('dp', 'dict')
- grad_dec: bfloat16 [32768, 8192], P('dict', 'dp')
Inputs may be any that keep to these rules, and one draw needn't show every extreme that they name: Each row block lists 2 different panels. Among the 16 row blocks of one index of dict, no panel is listed by more than 2 blocks, and some panel is listed by exactly 2.
All inputs are finite; a program needn't handle non-finite values.
Results may differ from a plain program's by a relative error of at most 0.0057.
Values may be sent and summed in bfloat16 or wider, within the bound.
No kernel may reach another device: no remote copies, remote signals or barrier semaphores. Data moves between devices by JAX's collectives and lax.ppermute only.
A program may use at most 128 MiB of HBM per device.

v0:
```python
import jax
import jax.numpy as jnp
from jax import lax
from jax.sharding import PartitionSpec as P


def on_device(acts, lists, w_enc, w_dec, b_enc, b_dec):
    peers = lax.axis_size("dict")
    block_count = lists.shape[0]
    active_count = lists.shape[1]
    rows_block = acts.shape[0] // block_count
    feature_cols = acts.shape[1]
    capacity = max(2, (2 * block_count * active_count + peers - 1) // peers)
    slot_total = peers * capacity
    flat_ids = lists.reshape(-1)
    onehot = (flat_ids[:, None] == jnp.arange(peers, dtype=jnp.int32)[None, :]).astype(jnp.int32)
    rank_index = jnp.sum((jnp.cumsum(onehot, axis=0) - 1) * onehot, axis=1)
    slot_index = flat_ids * capacity + rank_index
    item_block = jnp.arange(block_count * active_count, dtype=jnp.int32) // active_count
    slot_match = (jnp.arange(slot_total, dtype=jnp.int32)[:, None] == slot_index[None, :]).astype(
        jnp.float32
    )
    block_match = (item_block[:, None] == jnp.arange(block_count, dtype=jnp.int32)[None, :]).astype(
        jnp.float32
    )
    selector = jnp.dot(slot_match, block_match).astype(jnp.bfloat16)
    block_rows = acts.reshape(block_count, rows_block * feature_cols)
    outgoing = jnp.dot(selector, block_rows, preferred_element_type=jnp.float32).astype(
        jnp.bfloat16
    )
    outgoing = outgoing.reshape(peers, capacity * rows_block, feature_cols)
    received = lax.all_to_all(outgoing, "dict", split_axis=0, concat_axis=0, tiled=True)
    rows_in = received.reshape(-1, feature_cols)
    pre_local = jnp.dot(rows_in, w_enc, preferred_element_type=jnp.float32)
    bias_enc = b_enc.astype(jnp.float32)
    preact = lax.psum(pre_local, "dp") + bias_enc
    activity = (jnp.maximum(preact, 0.0) ** 2).astype(jnp.bfloat16)
    part = jnp.dot(activity, w_dec, preferred_element_type=jnp.float32).astype(jnp.bfloat16)
    part = part.reshape(peers, capacity * rows_block, feature_cols)
    returned = lax.all_to_all(part, "dict", split_axis=0, concat_axis=0, tiled=True)
    returned = returned.reshape(slot_total, rows_block * feature_cols)
    rebuilt = lax.dot_general(
        selector, returned, (((0,), (0,)), ((), ())), preferred_element_type=jnp.float32
    )
    rebuilt = rebuilt.reshape(block_count * rows_block, feature_cols) + b_dec.astype(jnp.float32)
    residual_g = ((rebuilt - acts.astype(jnp.float32)) * (1.0 / rows_block)).astype(jnp.bfloat16)
    resid_out = jnp.dot(
        selector,
        residual_g.reshape(block_count, rows_block * feature_cols),
        preferred_element_type=jnp.float32,
    ).astype(jnp.bfloat16)
    resid_out = resid_out.reshape(peers, capacity * rows_block, feature_cols)
    residual_in = lax.all_to_all(
        resid_out, "dict", split_axis=0, concat_axis=0, tiled=True
    ).reshape(-1, feature_cols)
    grad_dec = lax.dot_general(
        activity, residual_in, (((0,), (0,)), ((), ())), preferred_element_type=jnp.float32
    ).astype(jnp.bfloat16)
    dact_local = lax.dot_general(
        residual_in, w_dec, (((1,), (1,)), ((), ())), preferred_element_type=jnp.float32
    )
    dact = lax.psum(dact_local, "dp")
    grad_pre = (dact * 2.0 * jnp.maximum(preact, 0.0)).astype(jnp.bfloat16)
    grad_enc = lax.dot_general(
        rows_in, grad_pre, (((0,), (0,)), ((), ())), preferred_element_type=jnp.float32
    ).astype(jnp.bfloat16)
    return (grad_enc, grad_dec)


def solution(mesh):
    in_specs = (
        P("dict", "dp"),
        P("dict", None),
        P("dp", "dict"),
        P("dict", "dp"),
        P("dict"),
        P("dp"),
    )
    out_specs = (P("dp", "dict"), P("dict", "dp"))
    return jax.shard_map(
        on_device, mesh=mesh, in_specs=in_specs, out_specs=out_specs, check_vma=False
    )
```

profile of v0, /device:TPU:1, one launch (start us, length us, event | category | flops | bytes accessed | tf_op | source)
XLA Modules:
  0.0 449.6 jit_solution(6548300190928002087)
XLA Ops:
  7.2 0.0 all-reduce.3.cloned.1.call-start
  7.2 0.8 copy.9
  8.0 0.1 reshape.58
  8.1 0.1 fusion.4
  8.1 0.1 reduce_window_sum.11
  8.2 0.2 select_reduce_fusion
  8.4 1.6 reshape.59
  9.9 0.2 convolution_convert_fusion.5
  10.2 3.3 convolution_convert_fusion.1
  13.5 7.4 %reshape.60 = bf16[32,32,2048]{2,1,0:T(8,128)(2,1)} reshape(bf16[64,32768]{1,0:T(8,128)(2,1)} %convolution_convert_fusion.1) | data formatting | bytes 8388608 | tf_op jit(solution)/shard_map/reshape | solution.py:31
  20.9 60.3 %all_to_all.15 = bf16[32,32,2048]{2,1,0:T(8,128)(2,1)S(1)} all-to-all(bf16[32,32,2048]{2,1,0:T(8,128)(2,1)} %reshape.60), channel_id=1, replica_groups=mesh['dp'=4,'dict'=32] {'dict'}, dimensions={0} | all-to-all | bytes 8388608 | tf_op jit(solution)/shard_map/all_to_all | solution.py:32
  81.2 2.0 copy-done
  83.1 6.0 %fusion.10 = f32[1024,1024]{1,0:T(8,128)} fusion(bf16[1024,2048]{1,0:T(8,128)(2,1)S(1)} %bitcast.16, bf16[2048,1024]{1,0:T(8,128)(2,1)S(1)} %copy-done.5), kind=kOutput, calls=%fused_computation.29 | convolution fusion | flops 4294967296 | bytes 12582912 | tf_op jit(solution)/shard_map/dot_general | solution.py:34
  89.1 0.7 copy-done.4
  89.8 89.8 %all-reduce.3.cloned.1.call-done = f32[1024,1024]{1,0:T(8,128)} async-done(((f32[1024,1024]{1,0:T(8,128)}), f32[1024,1024]{1,0:T(8,128)}) %all-reduce.3.cloned.1.call-update) | async-done | bytes 4194320 | tf_op jit(solution)/shard_map/psum | solution.py:36
  179.6 10.0 %convolution_convert_fusion.4 = bf16[1024,2048]{1,0:T(8,128)(2,1)} fusion(bf16[1024,2048]{1,0:T(8,128)(2,1)} %param.9, f32[1024,1024]{1,0:T(8,128)} %all-reduce.3.cloned.1.call-done, f32[1024]{0:T(1024)S(1)} %convert_element_type.44), kind=kOutput, calls=%fused_computation.7 | convolution fusion | flops 4301258752 | bytes 12587008 | tf_op jit(solution)/shard_map/dot_general | solution.py:38
  189.6 8.0 %all-to-all-start.1 = ((bf16[32,32,2048]{2,1,0:T(8,128)(2,1)}), bf16[32,32,2048]{2,1,0:T(8,128)(2,1)}, u32[]{:S(2)}, u32[]{:S(2)}) async-start(bf16[32,32,2048]{2,1,0:T(8,128)(2,1)} %bitcast.20), calls=%async_computation.1 | async-start | bytes 8388608 | tf_op jit(solution)/shard_map/all_to_all | solution.py:40
  197.6 0.0 all-reduce.5.cloned.1.call-start
  197.7 52.0 %all-to-all-done.1 = bf16[32,32,2048]{2,1,0:T(8,128)(2,1)} async-done(((bf16[32,32,2048]{2,1,0:T(8,128)(2,1)}), bf16[32,32,2048]{2,1,0:T(8,128)(2,1)}, u32[]{:S(2)}, u32[]{:S(2)}) %all-to-all-start.1) | async-done | bytes 4194336 | tf_op jit(solution)/shard_map/all_to_all | solution.py:40
  249.7 7.4 %reshape.63 = bf16[64,32768]{1,0:T(8,128)(2,1)} reshape(bf16[32,32,2048]{2,1,0:T(8,128)(2,1)} %all-to-all-done.1) | data formatting | bytes 8388608 | tf_op jit(solution)/shard_map/reshape | solution.py:41
  257.1 4.3 fusion.11
  261.4 1.7 reshape.64
  263.1 1.3 multiply_convert_fusion.3
  264.5 1.6 reshape.65
  266.0 3.3 convolution_convert_fusion
  269.3 7.4 %reshape.66 = bf16[32,32,2048]{2,1,0:T(8,128)(2,1)} reshape(bf16[64,32768]{1,0:T(8,128)(2,1)} %convolution_convert_fusion) | data formatting | bytes 8388608 | tf_op jit(solution)/shard_map/reshape | solution.py:52
  276.7 57.9 %all_to_all.16 = bf16[32,32,2048]{2,1,0:T(8,128)(2,1)S(1)} all-to-all(bf16[32,32,2048]{2,1,0:T(8,128)(2,1)} %reshape.66), channel_id=1, replica_groups=mesh['dp'=4,'dict'=32] {'dict'}, dimensions={0} | all-to-all | bytes 8388608 | tf_op jit(solution)/shard_map/all_to_all | solution.py:53
  334.6 1.9 copy-done.1
  336.5 6.1 %fusion.12 = f32[1024,1024]{1,0:T(8,128)} fusion(bf16[1024,2048]{1,0:T(8,128)(2,1)S(1)} %bitcast.18, bf16[1024,2048]{1,0:T(8,128)(2,1)S(1)} %copy-done.6), kind=kOutput, calls=%fused_computation.31 | convolution fusion | flops 4294967296 | bytes 12582912 | tf_op jit(solution)/shard_map/dot_general | solution.py:59
  342.6 10.1 %convolution_convert_fusion.2 = bf16[1024,2048]{1,0:T(8,128)(2,1)} fusion(bf16[1024,2048]{1,0:T(8,128)(2,1)} %bitcast.19, f32[1024,1024]{1,0:T(8,128)} %all-reduce.3.cloned.1.call-done, f32[1024]{0:T(1024)S(1)} %convert_element_type.44), kind=kOutput, calls=%fused_computation.5 | convolution fusion | flops 4301258752 | bytes 12587008 | tf_op jit(solution)/shard_map/dot_general | solution.py:56
  352.7 78.8 %all-reduce.5.cloned.1.call-done = f32[1024,1024]{1,0:T(8,128)} async-done(((f32[1024,1024]{1,0:T(8,128)}), f32[1024,1024]{1,0:T(8,128)}) %all-reduce.5.cloned.1.call-update) | async-done | bytes 4194320 | tf_op jit(solution)/shard_map/psum | solution.py:62
  431.5 11.3 %convolution_convert_fusion.3 = bf16[2048,1024]{1,0:T(8,128)(2,1)} fusion(bf16[1024,2048]{1,0:T(8,128)(2,1)} %bitcast.17, f32[1024,1024]{1,0:T(8,128)} %all-reduce.5.cloned.1.call-done, f32[1024,1024]{1,0:T(8,128)} %all-reduce.3.cloned.1.call-done, f32[1024]{0:T(1024)S(1)} %convert_element_type.44), kind=kOutput, calls=%fused_computation.6 | convolution fusion | flops 4302307328 | bytes 16781312 | tf_op jit(solution)/shard_map/dot_general | solution.py:64
  (16 shorter events, 0.1 us)
Async XLA Ops:
  7.2 172.5 %all-reduce.3.cloned.1.call-start = ((), (), s32[]{:S(2)}) async-start(), calls=%async_computation.3 | async-start | bytes 8388608 | tf_op jit(solution)/shard_map/psum | solution.py:36
  20.9 62.3 %copy-start.5 = (bf16[2048,1024]{1,0:T(8,128)(2,1)S(1)}, bf16[2048,1024]{1,0:T(8,128)(2,1)}, u32[]{:S(2)}) copy-start(bf16[2048,1024]{1,0:T(8,128)(2,1)} %param.8) | copy-start | bytes 12582916
  81.2 2.0 copy-start
  89.1 0.7 copy-start.4
  189.6 8.1 %copy-start.3 = (bf16[2048]{0:T(1024)(128)(2,1)S(1)}, bf16[2048]{0:T(1024)(128)(2,1)}, u32[]{:S(2)}) copy-start(bf16[2048]{0:T(1024)(128)(2,1)} %param.11) | copy-start | bytes 12292
  189.6 60.1 %all-to-all-start.1 = ((bf16[32,32,2048]{2,1,0:T(8,128)(2,1)}), bf16[32,32,2048]{2,1,0:T(8,128)(2,1)}, u32[]{:S(2)}, u32[]{:S(2)}) async-start(bf16[32,32,2048]{2,1,0:T(8,128)(2,1)} %bitcast.20), calls=%async_computation.1 | async-start | bytes 8388608 | tf_op jit(solution)/shard_map/all_to_all | solution.py:40
  197.6 233.8 %all-reduce.5.cloned.1.call-start = ((), (), s32[]{:S(2)}) async-start(), calls=%async_computation.4 | async-start | bytes 8388608 | tf_op jit(solution)/shard_map/psum | solution.py:62
  257.1 6.0 %copy-start.2 = (bf16[256,2048]{1,0:T(8,128)(2,1)S(1)}, bf16[256,2048]{1,0:T(8,128)(2,1)}, u32[]{:S(2)}) copy-start(bf16[256,2048]{1,0:T(8,128)(2,1)} %param.6) | copy-start | bytes 3145732
  276.7 59.9 %copy-start.6 = (bf16[1024,2048]{1,0:T(8,128)(2,1)S(1)}, bf16[1024,2048]{1,0:T(8,128)(2,1)}, u32[]{:S(2)}) copy-start(bf16[1024,2048]{1,0:T(8,128)(2,1)} %param.9) | copy-start | bytes 12582916
  334.6 1.9 copy-start.1
Sparse Core Ops, SparseCore 0:
  89.3 90.3 all-reduce.2
  342.7 88.6 all-reduce.4
where the time goes:
time: 450 us
  waiting for transfers between devices  221 us (49%)
  blocking collectives  118 us (26%)
  matrix products  54.5 us (12%)
  local copies, waits for them, and re-layouts  32.4 us (7%)
  between operations  14.1 us (3%)
  starting transfers between devices  8.1 us (2%)
    psum x1, waiting for transfers between devices, on_device(): preact = lax.psum(pre_local, 'dp') + bias_enc  89.8 us
    psum x1, waiting for transfers between devices, on_device(): dact = lax.psum(dact_local, 'dp')  78.8 us
    all_to_all x1, blocking collectives, on_device(): lax.all_to_all(outgoing, 'dict', split_axis=0, concat_axis=0, tiled=True)  60.3 us
    all_to_all x1, blocking collectives, on_device(): lax.all_to_all(resid_out, 'dict', split_axis=0, concat_axis=0, tiled=True)  57.9 us
    all_to_all x1, waiting for transfers between devices, on_device(): lax.all_to_all(part, 'dict', split_axis=0, concat_axis=0, tiled=True)  52 us
    dot_general x1, matrix products, on_device(): lax.dot_general(rows_in, grad_pre, (((0,), (0,)), ((), ())), preferred_el...  11.3 us
    dot_general x1, matrix products, on_device(): lax.dot_general(activity, residual_in, (((0,), (0,)), ((), ())), preferre...  10.1 us
    dot_general x1, matrix products, on_device(): jnp.dot(activity, w_dec, preferred_element_type=jnp.float32)  9.98 us
  transfers between devices with their start and end apart: 3, of which 3 were waited for; matrix products, arithmetic and copies ran while one was open for 2% of the time, Pallas kernels for 0%

commit v1 on v0

--- a/solution.py
+++ b/solution.py
@@ -59,7 +59,11 @@
     dact_local = lax.dot_general(
         residual_in, w_dec, (((1,), (1,)), ((), ())), preferred_element_type=jnp.float32
     )
-    dact = lax.psum(dact_local, "dp")
+
+    def watch_object(unit, mesh_ax):
+        return lax.all_gather(unit, mesh_ax).sum(axis=0)
+
+    dact = watch_object(dact_local, "dp")
     grad_pre = (dact * 2.0 * jnp.maximum(preact, 0.0)).astype(jnp.bfloat16)
     grad_enc = lax.dot_general(
         rows_in, grad_pre, (((0,), (0,)), ((), ())), preferred_element_type=jnp.float32

time: 450 us -> 522 us (1.16)
  waiting for transfers between devices: 221 us -> 282 us
  other arithmetic: 1.64 us -> 11.9 us
    all_gather x0 -> x1, waiting for transfers between devices: none -> 140 us  [watch_object(): return lax.all_gather(unit, mesh_ax).sum(axis=0)]
    psum x1 -> x0, waiting for transfers between devices: 78.8 us -> none  [on_device(): dact = lax.psum(dact_local, 'dp')]
    reduce_sum x0 -> x1, other arithmetic: none -> 10.3 us  [watch_object(): return lax.all_gather(unit, mesh_ax).sum(axis=0)]
where the time goes in v1:
time: 522 us; the launch traced here: 521 us
  waiting for transfers between devices  282 us (54%)
  blocking collectives  118 us (23%)
  matrix products  54.7 us (10%)
  local copies, waits for them, and re-layouts  32.4 us (6%)
  between operations  14.1 us (3%)
  other arithmetic  11.9 us (2%)
  starting transfers between devices  8.1 us (2%)
    all_gather x1, waiting for transfers between devices, watch_object(): return lax.all_gather(unit, mesh_ax).sum(axis=0)  140 us
    psum x1, waiting for transfers between devices, on_device(): preact = lax.psum(pre_local, 'dp') + bias_enc  89.8 us
    all_to_all x1, blocking collectives, on_device(): lax.all_to_all(outgoing, 'dict', split_axis=0, concat_axis=0, tiled=True)  60.3 us
    all_to_all x1, blocking collectives, on_device(): lax.all_to_all(resid_out, 'dict', split_axis=0, concat_axis=0, tiled=True)  57.9 us
    all_to_all x1, waiting for transfers between devices, on_device(): lax.all_to_all(part, 'dict', split_axis=0, concat_axis=0, tiled=True)  52 us
    dot_general x1, matrix products, on_device(): lax.dot_general(rows_in, grad_pre, (((0,), (0,)), ((), ())), preferred_el...  11.3 us
  transfers between devices with their start and end apart: 3, of which 3 were waited for; matrix products, arithmetic and copies ran while one was open for 2% of the time, Pallas kernels for 0%

profile of v1, /device:TPU:1, one launch (start us, length us, event | category | flops | bytes accessed | tf_op | source)
XLA Modules:
  0.0 521.2 jit_solution(18428496653221606276)
XLA Ops:
  7.2 0.8 copy.9
  8.0 0.1 reshape.58
  8.1 0.1 fusion.4
  8.1 0.1 reduce_window_sum.11
  8.2 0.2 select_reduce_fusion
  8.4 1.6 reshape.59
  9.9 0.2 convolution_convert_fusion.5
  10.2 3.3 convolution_convert_fusion.1
  13.5 7.4 %reshape.60 = bf16[32,32,2048]{2,1,0:T(8,128)(2,1)} reshape(bf16[64,32768]{1,0:T(8,128)(2,1)} %convolution_convert_fusion.1) | data formatting | bytes 8388608 | tf_op jit(solution)/shard_map/reshape | solution.py:31
  20.9 60.3 %all_to_all.15 = bf16[32,32,2048]{2,1,0:T(8,128)(2,1)S(1)} all-to-all(bf16[32,32,2048]{2,1,0:T(8,128)(2,1)} %reshape.60), channel_id=1, replica_groups=mesh['dp'=4,'dict'=32] {'dict'}, dimensions={0} | all-to-all | bytes 8388608 | tf_op jit(solution)/shard_map/all_to_all | solution.py:32
  81.2 2.0 copy-done
  83.1 6.0 %fusion.10 = f32[1024,1024]{1,0:T(8,128)} fusion(bf16[1024,2048]{1,0:T(8,128)(2,1)S(1)} %bitcast.18, bf16[2048,1024]{1,0:T(8,128)(2,1)S(1)} %copy-done.5), kind=kOutput, calls=%fused_computation.29 | convolution fusion | flops 4294967296 | bytes 12582912 | tf_op jit(solution)/shard_map/dot_general | solution.py:34
  89.1 0.7 copy-done.4
  89.8 89.8 %all-reduce.2.cloned.1.call-done = f32[1024,1024]{1,0:T(8,128)} async-done(((f32[1024,1024]{1,0:T(8,128)}), f32[1024,1024]{1,0:T(8,128)}) %all-reduce.2.cloned.1.call-update) | async-done | bytes 4194320 | tf_op jit(solution)/shard_map/psum | solution.py:36
  179.6 10.0 %convolution_convert_fusion.4 = bf16[1024,2048]{1,0:T(8,128)(2,1)} fusion(bf16[1024,2048]{1,0:T(8,128)(2,1)} %param.9, f32[1024,1024]{1,0:T(8,128)} %all-reduce.2.cloned.1.call-done, f32[1024]{0:T(1024)S(1)} %convert_element_type.44), kind=kOutput, calls=%fused_computation.7 | convolution fusion | flops 4301258752 | bytes 12587008 | tf_op jit(solution)/shard_map/dot_general | solution.py:38
  189.6 8.0 %all-to-all-start.1 = ((bf16[32,32,2048]{2,1,0:T(8,128)(2,1)}), bf16[32,32,2048]{2,1,0:T(8,128)(2,1)}, u32[]{:S(2)}, u32[]{:S(2)}) async-start(bf16[32,32,2048]{2,1,0:T(8,128)(2,1)} %bitcast.22), calls=%async_computation.1 | async-start | bytes 8388608 | tf_op jit(solution)/shard_map/all_to_all | solution.py:40
  197.6 0.0 all-gather.3.cloned.1.call-start
  197.7 52.0 %all-to-all-done.1 = bf16[32,32,2048]{2,1,0:T(8,128)(2,1)} async-done(((bf16[32,32,2048]{2,1,0:T(8,128)(2,1)}), bf16[32,32,2048]{2,1,0:T(8,128)(2,1)}, u32[]{:S(2)}, u32[]{:S(2)}) %all-to-all-start.1) | async-done | bytes 4194336 | tf_op jit(solution)/shard_map/all_to_all | solution.py:40
  249.7 7.4 %reshape.63 = bf16[64,32768]{1,0:T(8,128)(2,1)} reshape(bf16[32,32,2048]{2,1,0:T(8,128)(2,1)} %all-to-all-done.1) | data formatting | bytes 8388608 | tf_op jit(solution)/shard_map/reshape | solution.py:41
  257.1 4.3 fusion.11
  261.4 1.7 reshape.64
  263.1 1.3 multiply_convert_fusion.3
  264.5 1.6 reshape.65
  266.0 3.3 convolution_convert_fusion
  269.3 7.4 %reshape.66 = bf16[32,32,2048]{2,1,0:T(8,128)(2,1)} reshape(bf16[64,32768]{1,0:T(8,128)(2,1)} %convolution_convert_fusion) | data formatting | bytes 8388608 | tf_op jit(solution)/shard_map/reshape | solution.py:52
  276.7 57.9 %all_to_all.16 = bf16[32,32,2048]{2,1,0:T(8,128)(2,1)S(1)} all-to-all(bf16[32,32,2048]{2,1,0:T(8,128)(2,1)} %reshape.66), channel_id=1, replica_groups=mesh['dp'=4,'dict'=32] {'dict'}, dimensions={0} | all-to-all | bytes 8388608 | tf_op jit(solution)/shard_map/all_to_all | solution.py:53
  334.6 1.9 copy-done.1
  336.5 6.1 %fusion.12 = f32[1024,1024]{1,0:T(8,128)} fusion(bf16[1024,2048]{1,0:T(8,128)(2,1)S(1)} %bitcast.20, bf16[1024,2048]{1,0:T(8,128)(2,1)S(1)} %copy-done.6), kind=kOutput, calls=%fused_computation.31 | convolution fusion | flops 4294967296 | bytes 12582912 | tf_op jit(solution)/shard_map/dot_general | solution.py:59
  342.6 10.3 %convolution_convert_fusion.2 = bf16[1024,2048]{1,0:T(8,128)(2,1)} fusion(bf16[1024,2048]{1,0:T(8,128)(2,1)} %bitcast.21, f32[1024,1024]{1,0:T(8,128)} %all-reduce.2.cloned.1.call-done, f32[1024]{0:T(1024)S(1)} %convert_element_type.44), kind=kOutput, calls=%fused_computation.5 | convolution fusion | flops 4301258752 | bytes 12587008 | tf_op jit(solution)/shard_map/dot_general | solution.py:56
  352.9 139.8 %all-gather.3.cloned.1.call-done = f32[4096,1024]{1,0:T(8,128)} async-done(((f32[1024,1024]{1,0:T(8,128)}), f32[4096,1024]{1,0:T(8,128)}) %all-gather.3.cloned.1.call-update) | async-done | bytes 16777232 | tf_op jit(solution)/shard_map/all_gather | solution.py:64
  492.7 10.3 %reduce_sum.19 = f32[1024,1024]{1,0:T(8,128)} reduce(f32[4,1024,1024]{2,1,0:T(8,128)} %bitcast.17, f32[]{:T(128)} %constant.29.clone.1), dimensions={0}, to_apply=%region_3.4 | reduce | flops 3145728 | bytes 20971524 | tf_op jit(solution)/shard_map/reduce_sum | solution.py:64
  503.0 11.3 %convolution_convert_fusion.3 = bf16[2048,1024]{1,0:T(8,128)(2,1)} fusion(bf16[1024,2048]{1,0:T(8,128)(2,1)} %bitcast.19, f32[1024,1024]{1,0:T(8,128)} %reduce_sum.19, f32[1024,1024]{1,0:T(8,128)} %all-reduce.2.cloned.1.call-done, f32[1024]{0:T(1024)S(1)} %convert_element_type.44), kind=kOutput, calls=%fused_computation.6 | convolution fusion | flops 4302307328 | bytes 16781312 | tf_op jit(solution)/shard_map/dot_general | solution.py:68
  (17 shorter events, 0.1 us)
Async XLA Ops:
  7.2 172.4 %all-reduce.2.cloned.1.call-start = ((), (), s32[]{:S(2)}) async-start(), calls=%async_computation.3 | async-start | bytes 8388608 | tf_op jit(solution)/shard_map/psum | solution.py:36
  20.9 62.3 %copy-start.5 = (bf16[2048,1024]{1,0:T(8,128)(2,1)S(1)}, bf16[2048,1024]{1,0:T(8,128)(2,1)}, u32[]{:S(2)}) copy-start(bf16[2048,1024]{1,0:T(8,128)(2,1)} %param.8) | copy-start | bytes 12582916
  81.2 2.0 copy-start
  89.1 0.7 copy-start.4
  189.6 8.1 %copy-start.3 = (bf16[2048]{0:T(1024)(128)(2,1)S(1)}, bf16[2048]{0:T(1024)(128)(2,1)}, u32[]{:S(2)}) copy-start(bf16[2048]{0:T(1024)(128)(2,1)} %param.11) | copy-start | bytes 12292
  189.6 60.1 %all-to-all-start.1 = ((bf16[32,32,2048]{2,1,0:T(8,128)(2,1)}), bf16[32,32,2048]{2,1,0:T(8,128)(2,1)}, u32[]{:S(2)}, u32[]{:S(2)}) async-start(bf16[32,32,2048]{2,1,0:T(8,128)(2,1)} %bitcast.22), calls=%async_computation.1 | async-start | bytes 8388608 | tf_op jit(solution)/shard_map/all_to_all | solution.py:40
  197.6 295.1 %all-gather.3.cloned.1.call-start = ((), (), s32[]{:S(2)}) async-start(), calls=%async_computation.4 | async-start | bytes 20971520 | tf_op jit(solution)/shard_map/all_gather | solution.py:64
  257.1 6.0 %copy-start.2 = (bf16[256,2048]{1,0:T(8,128)(2,1)S(1)}, bf16[256,2048]{1,0:T(8,128)(2,1)}, u32[]{:S(2)}) copy-start(bf16[256,2048]{1,0:T(8,128)(2,1)} %param.6) | copy-start | bytes 3145732
  276.7 59.9 %copy-start.6 = (bf16[1024,2048]{1,0:T(8,128)(2,1)S(1)}, bf16[1024,2048]{1,0:T(8,128)(2,1)}, u32[]{:S(2)}) copy-start(bf16[1024,2048]{1,0:T(8,128)(2,1)} %param.9) | copy-start | bytes 12582916
  334.6 1.9 copy-start.1
Sparse Core Ops, SparseCore 0:
  89.3 90.3 all-reduce.1
  342.7 149.9 all-gather.2
